TPU v7x, 512 devices: a whole 4x4x16 slice. The times are simulated.
512 devices in a mesh: gx: 8 (over y, core), gy: 4 (over x), gz: 16 (over z).
Axes of the slice: x: 4, y: 4, z: 16, core: 2. Of those that a mesh axis runs over, the one named last changes fastest.
Arguments:
- level_set: float32 [128, 64, 2048], P('gx', 'gy', 'gz'), may hold values from 0 to 1
- velocity: float32 [3, 128, 64, 2048], P(None, 'gx', 'gy', 'gz'), may hold values from -6 to 6
- source: float32 [128, 64, 2048], P('gx', 'gy', 'gz'), may hold values from -6 to 6
- coarse_factor: float32 [512, 512], P(('gx', 'gy', 'gz')), may hold values from -0.2 to 0.2
Outputs:
- level_set_new: float32 [128, 64, 2048], P('gx', 'gy', 'gz')
- pressure: float32 [128, 64, 2048], P('gx', 'gy', 'gz')
All inputs are finite; a program needn't handle non-finite values.
Results may differ from a plain program's by a relative error of at most 0.029.
Values sent between devices are 32-bit elements; how exact they have to be, the bound alone decides.
A program may use at most 64 MiB of HBM per device.

v0:
```python
import jax
import jax.numpy as jnp
import numpy as np
from jax import lax
from jax.sharding import PartitionSpec as P

NP = 8
RSWEEPS = 2
ITERS = 6
GLL_POINTS = (
    -1.0,
    -0.8717401485096066,
    -0.5917001814331423,
    -0.2092992179024789,
    0.2092992179024789,
    0.5917001814331423,
    0.8717401485096066,
    1.0,
)
GLL_WEIGHTS = (
    0.03571428571428571,
    0.21070422714350603,
    0.3411226924835044,
    0.4124587946587038,
    0.4124587946587038,
    0.3411226924835044,
    0.21070422714350603,
    0.03571428571428571,
)
HIGHEST = lax.Precision.HIGHEST
TIME_STEP = 0.02
PSEUDO_STEP = 0.004
INTERFACE_WIDTH = 0.5
GAS_DENSITY = 0.1
SOURCE_SCALE = 20.0


def extended(cells, sides, width):
    for axis, dim in sides:
        count = lax.axis_size(axis)
        ends = count - 1
        head = lax.slice_in_dim(cells, 0, width, axis=dim)
        tail = lax.slice_in_dim(cells, cells.shape[dim] - width, cells.shape[dim], axis=dim)
        cells = jnp.concatenate(
            [
                lax.ppermute(tail, axis, [(i, (i + 1) % count) for i in range(ends)]),
                cells,
                lax.ppermute(head, axis, [((i + 1) % count, i) for i in range(ends)]),
            ],
            axis=dim,
        )
    return cells


def node_tables():
    points = np.array(GLL_POINTS)
    amount = points.shape[0]
    barycentric = np.ones(amount)
    for target in range(amount):
        for partner in range(amount):
            if partner != target:
                barycentric[target] = barycentric[target] / (points[target] - points[partner])
    derivative = np.zeros((amount, amount))
    for target in range(amount):
        for partner in range(amount):
            if partner != target:
                derivative[target, partner] = (
                    barycentric[partner] / barycentric[target] / (points[target] - points[partner])
                )
        derivative[target, target] = -np.sum(derivative[target])
    return derivative


def apply_axis(values, matrix, which_axis):
    if which_axis == 0:
        return jnp.einsum("ap,pqr->aqr", matrix, values, precision=HIGHEST)
    if which_axis == 1:
        return jnp.einsum("aq,pqr->par", matrix, values, precision=HIGHEST)
    return jnp.einsum("pqr,ar->pqa", values, matrix, precision=HIGHEST)


def edge_passes(padded):
    summed = padded
    for which_axis in (1, 2, 3):
        amount = summed.shape[which_axis] - 2
        center = lax.slice_in_dim(summed, 1, amount + 1, axis=which_axis)
        upper_side = lax.slice_in_dim(summed, 2, amount + 2, axis=which_axis)
        lower_side = lax.slice_in_dim(summed, 0, amount, axis=which_axis)
        shape_list = [1, 1, 1, 1]
        shape_list[which_axis] = amount
        position = (jnp.arange(amount) % NP).reshape(shape_list)
        summed = (
            center
            + jnp.where(position == NP - 1, upper_side, 0.0)
            + jnp.where(position == 0, lower_side, 0.0)
        )
    return summed


def assemble(stacked):
    padded = extended(stacked, (("gx", 1), ("gy", 2), ("gz", 3)), 1)
    return edge_passes(padded)


def body(level_set, velocity, source, coarse_factor):
    shape_tuple = level_set.shape
    derivative = node_tables()
    deriv_tables = [
        jnp.asarray(np.kron(np.eye(extent // NP), derivative), jnp.float32)
        for extent in shape_tuple
    ]
    trans_tables = [
        jnp.asarray(np.kron(np.eye(extent // NP), derivative.T), jnp.float32)
        for extent in shape_tuple
    ]
    square_tables = [
        jnp.asarray(np.kron(np.eye(extent // NP), (derivative * derivative).T), jnp.float32)
        for extent in shape_tuple
    ]
    weights = jnp.asarray(np.array(GLL_WEIGHTS), jnp.float32)
    along_x = jnp.tile(weights, shape_tuple[0] // NP)
    along_y = jnp.tile(weights, shape_tuple[1] // NP)
    along_z = jnp.tile(weights, shape_tuple[2] // NP)
    bmass = along_x[:, None, None] * along_y[None, :, None] * along_z[None, None, :]
    gradient = [
        apply_axis(level_set, deriv_tables[which_axis], which_axis) for which_axis in range(3)
    ]
    advect = velocity[0] * gradient[0] + velocity[1] * gradient[1] + velocity[2] * gradient[2]
    divergence = (
        apply_axis(bmass * velocity[0], trans_tables[0], 0)
        + apply_axis(bmass * velocity[1], trans_tables[1], 1)
        + apply_axis(bmass * velocity[2], trans_tables[2], 2)
        + bmass * source
    )
    assembled = assemble(jnp.stack([bmass * advect, bmass, divergence]))
    mass_sum = assembled[1]
    weight = bmass / mass_sum
    level_now = level_set - TIME_STEP * assembled[0] / mass_sum
    rhs_field = SOURCE_SCALE * assembled[2]
    for sweep in range(RSWEEPS):
        gradient = [
            apply_axis(level_now, deriv_tables[which_axis], which_axis) for which_axis in range(3)
        ]
        inv_norm = 1.0 / jnp.sqrt(
            1.0 + gradient[0] * gradient[0] + gradient[1] * gradient[1] + gradient[2] * gradient[2]
        )
        compress = level_now * (1.0 - level_now) * inv_norm
        weak_form = apply_axis(
            bmass * (compress * gradient[0] - INTERFACE_WIDTH * gradient[0]), trans_tables[0], 0
        )
        weak_form = weak_form + apply_axis(
            bmass * (compress * gradient[1] - INTERFACE_WIDTH * gradient[1]), trans_tables[1], 1
        )
        weak_form = weak_form + apply_axis(
            bmass * (compress * gradient[2] - INTERFACE_WIDTH * gradient[2]), trans_tables[2], 2
        )
        level_now = level_now + PSEUDO_STEP * assemble(weak_form[None])[0] / mass_sum
    inverse_density = 1.0 / (GAS_DENSITY + (1.0 - GAS_DENSITY) * jnp.clip(level_now, 0.0, 1.0))
    scaled = bmass * inverse_density
    diag_local = (
        apply_axis(scaled, square_tables[0], 0)
        + apply_axis(scaled, square_tables[1], 1)
        + apply_axis(scaled, square_tables[2], 2)
        + bmass
    )
    diagonal = assemble(diag_local[None])[0]
    own_row = coarse_factor[0]

    def precondition(residual):
        jacobi = residual / diagonal
        restricted = jnp.sum(weight * residual)
        coarse_mid = lax.psum(restricted * own_row, ("gx", "gy", "gz"))
        coarse_value = jnp.dot(own_row, coarse_mid, precision=HIGHEST)
        result = jacobi + assemble((weight * coarse_value)[None])[0]
        return (result, lax.psum(jnp.sum(weight * residual * result), ("gx", "gy", "gz")))

    pressure = jnp.zeros_like(rhs_field)
    residual = rhs_field
    direction, inner_now = precondition(residual)
    for step in range(ITERS):
        local_part = bmass * direction
        for element_which_axis in range(3):
            local_part = local_part + apply_axis(
                scaled
                * apply_axis(direction, deriv_tables[element_which_axis], element_which_axis),
                trans_tables[element_which_axis],
                element_which_axis,
            )
        image = assemble(local_part[None])[0]
        curvature = lax.psum(jnp.sum(weight * direction * image), ("gx", "gy", "gz"))
        step_size = inner_now / curvature
        pressure = pressure + step_size * direction
        residual = residual - step_size * image
        if step + 1 < ITERS:
            preconditioned, inner_next = precondition(residual)
            direction = preconditioned + inner_next / inner_now * direction
            inner_now = inner_next
    return (level_now, pressure)


def solution(mesh):
    in_specs = (
        P("gx", "gy", "gz"),
        P(None, "gx", "gy", "gz"),
        P("gx", "gy", "gz"),
        P(("gx", "gy", "gz"), None),
    )
    out_specs = (P("gx", "gy", "gz"), P("gx", "gy", "gz"))
    return jax.shard_map(body, mesh=mesh, in_specs=in_specs, out_specs=out_specs, check_vma=False)
```

profile of v0, /device:TPU:1, one launch (start us, length us, event | category | flops | bytes accessed | tf_op | source)
XLA Modules:
  0.0 2206.5 jit_solution(12459862347474892173)
XLA Ops:
  6.2 4.6 collective-permute-start
  10.8 5.5 collective-permute-start.1
  63.5 5.4 collective-permute-done.11
  87.6 4.9 collective-permute-start.16
  103.5 104.3 %psum.126 = f32[512]{0:T(512)S(1)} all-reduce(f32[512]{0:T(512)S(1)} %broadcast_multiply_fusion.13), channel_id=1, replica_groups=mesh['gx'=8,'gy'=4,'gz'=16] {'gx','gy','gz'}, use_global_device_ids=true, to_apply=%region_1.2 | all-reduce | flops 512 | bytes 4096 | tf_op jit(solution)/shard_map/psum | solution.py:172
  240.6 4.4 collective-permute-done.23
  256.2 4.3 collective-permute-start.32
  273.4 4.8 collective-permute-done.35
  279.6 104.5 %all-reduce = (f32[]{:T(128)}, f32[]{:T(128)}) all-reduce(f32[]{:T(128)} %get-tuple-element.9, f32[]{:T(128)} %get-tuple-element.8), channel_id=1, replica_groups=mesh['gx'=8,'gy'=4,'gz'=16] {'gx','gy','gz'}, use_global_device_ids=true, to_apply=%region_3.4 | all-reduce | flops 2 | bytes 16 | tf_op jit(solution)/shard_map/psum | solution.py:175
  386.8 98.4 %psum.129 = f32[512]{0:T(512)S(1)} all-reduce(f32[512]{0:T(512)S(1)} %broadcast_multiply_fusion.12), channel_id=1, replica_groups=mesh['gx'=8,'gy'=4,'gz'=16] {'gx','gy','gz'}, use_global_device_ids=true, to_apply=%region_7.8 | all-reduce | flops 512 | bytes 4096 | tf_op jit(solution)/shard_map/psum | solution.py:172
  514.5 101.3 %psum.130 = f32[]{:T(128)} all-reduce(f32[]{:T(128)} %get-tuple-element.36), channel_id=1, replica_groups=mesh['gx'=8,'gy'=4,'gz'=16] {'gx','gy','gz'}, use_global_device_ids=true, to_apply=%region_9.10 | all-reduce | flops 1 | bytes 8 | tf_op jit(solution)/shard_map/psum | solution.py:175
  645.7 102.2 %psum.131 = f32[]{:T(128)} all-reduce(f32[]{:T(128)} %get-tuple-element.34), channel_id=1, replica_groups=mesh['gx'=8,'gy'=4,'gz'=16] {'gx','gy','gz'}, use_global_device_ids=true, to_apply=%region_11.12 | all-reduce | flops 1 | bytes 8 | tf_op jit(solution)/shard_map/psum | solution.py:190
  750.5 99.1 %psum.132 = f32[512]{0:T(512)S(1)} all-reduce(f32[512]{0:T(512)S(1)} %broadcast_multiply_fusion.11), channel_id=1, replica_groups=mesh['gx'=8,'gy'=4,'gz'=16] {'gx','gy','gz'}, use_global_device_ids=true, to_apply=%region_13.14 | all-reduce | flops 512 | bytes 4096 | tf_op jit(solution)/shard_map/psum | solution.py:172
  879.3 100.7 %psum.133 = f32[]{:T(128)} all-reduce(f32[]{:T(128)} %get-tuple-element.30), channel_id=1, replica_groups=mesh['gx'=8,'gy'=4,'gz'=16] {'gx','gy','gz'}, use_global_device_ids=true, to_apply=%region_15.16 | all-reduce | flops 1 | bytes 8 | tf_op jit(solution)/shard_map/psum | solution.py:175
  1009.8 102.3 %psum.134 = f32[]{:T(128)} all-reduce(f32[]{:T(128)} %get-tuple-element.28), channel_id=1, replica_groups=mesh['gx'=8,'gy'=4,'gz'=16] {'gx','gy','gz'}, use_global_device_ids=true, to_apply=%region_17.18 | all-reduce | flops 1 | bytes 8 | tf_op jit(solution)/shard_map/psum | solution.py:190
  1114.7 98.7 %psum.135 = f32[512]{0:T(512)S(1)} all-reduce(f32[512]{0:T(512)S(1)} %broadcast_multiply_fusion.10), channel_id=1, replica_groups=mesh['gx'=8,'gy'=4,'gz'=16] {'gx','gy','gz'}, use_global_device_ids=true, to_apply=%region_19.20 | all-reduce | flops 512 | bytes 4096 | tf_op jit(solution)/shard_map/psum | solution.py:172
  1243.1 100.7 %psum.136 = f32[]{:T(128)} all-reduce(f32[]{:T(128)} %get-tuple-element.24), channel_id=1, replica_groups=mesh['gx'=8,'gy'=4,'gz'=16] {'gx','gy','gz'}, use_global_device_ids=true, to_apply=%region_21.22 | all-reduce | flops 1 | bytes 8 | tf_op jit(solution)/shard_map/psum | solution.py:175
  1373.6 102.5 %psum.137 = f32[]{:T(128)} all-reduce(f32[]{:T(128)} %get-tuple-element.22), channel_id=1, replica_groups=mesh['gx'=8,'gy'=4,'gz'=16] {'gx','gy','gz'}, use_global_device_ids=true, to_apply=%region_23.24 | all-reduce | flops 1 | bytes 8 | tf_op jit(solution)/shard_map/psum | solution.py:190
  1478.7 98.7 %psum.138 = f32[512]{0:T(512)S(1)} all-reduce(f32[512]{0:T(512)S(1)} %broadcast_multiply_fusion.9), channel_id=1, replica_groups=mesh['gx'=8,'gy'=4,'gz'=16] {'gx','gy','gz'}, use_global_device_ids=true, to_apply=%region_25.26 | all-reduce | flops 512 | bytes 4096 | tf_op jit(solution)/shard_map/psum | solution.py:172
  1607.0 100.7 %psum.139 = f32[]{:T(128)} all-reduce(f32[]{:T(128)} %get-tuple-element.18), channel_id=1, replica_groups=mesh['gx'=8,'gy'=4,'gz'=16] {'gx','gy','gz'}, use_global_device_ids=true, to_apply=%region_27.28 | all-reduce | flops 1 | bytes 8 | tf_op jit(solution)/shard_map/psum | solution.py:175
  1737.5 102.3 %psum.140 = f32[]{:T(128)} all-reduce(f32[]{:T(128)} %get-tuple-element.16), channel_id=1, replica_groups=mesh['gx'=8,'gy'=4,'gz'=16] {'gx','gy','gz'}, use_global_device_ids=true, to_apply=%region_29.30 | all-reduce | flops 1 | bytes 8 | tf_op jit(solution)/shard_map/psum | solution.py:190
  1842.5 98.7 %psum.141 = f32[512]{0:T(512)S(1)} all-reduce(f32[512]{0:T(512)S(1)} %broadcast_multiply_fusion.8), channel_id=1, replica_groups=mesh['gx'=8,'gy'=4,'gz'=16] {'gx','gy','gz'}, use_global_device_ids=true, to_apply=%region_31.32 | all-reduce | flops 512 | bytes 4096 | tf_op jit(solution)/shard_map/psum | solution.py:172
  1970.8 100.7 %psum.142 = f32[]{:T(128)} all-reduce(f32[]{:T(128)} %get-tuple-element.12), channel_id=1, replica_groups=mesh['gx'=8,'gy'=4,'gz'=16] {'gx','gy','gz'}, use_global_device_ids=true, to_apply=%region_33.34 | all-reduce | flops 1 | bytes 8 | tf_op jit(solution)/shard_map/psum | solution.py:175
  2102.2 102.1 %psum.143 = f32[]{:T(128)} all-reduce(f32[]{:T(128)} %fusion.92), channel_id=1, replica_groups=mesh['gx'=8,'gy'=4,'gz'=16] {'gx','gy','gz'}, use_global_device_ids=true, to_apply=%region_35.36 | all-reduce | flops 1 | bytes 8 | tf_op jit(solution)/shard_map/psum | solution.py:190
  (437 shorter events, 436.9 us)
Async XLA Ops:
  6.2 10.1 collective-permute-start
  54.7 8.8 collective-permute-start.10
  58.3 10.6 collective-permute-start.11
  87.6 10.1 collective-permute-start.16
  92.5 9.1 collective-permute-start.17
  209.1 10.4 collective-permute-start.24
  214.4 8.8 collective-permute-start.18
  219.6 9.2 collective-permute-start.26
  231.8 8.8 collective-permute-start.22
  235.7 9.3 collective-permute-start.23
  268.2 10.0 collective-permute-start.35
  500.5 8.7 collective-permute-start.40
  504.2 8.9 collective-permute-start.41
  635.3 9.1 collective-permute-start.47
  865.3 8.7 collective-permute-start.52
  869.0 8.9 collective-permute-start.53
  999.4 9.1 collective-permute-start.59
  1229.1 8.7 collective-permute-start.64
  1232.8 8.9 collective-permute-start.65
  1363.2 9.1 collective-permute-start.71
  1596.8 8.9 collective-permute-start.77
  1727.1 9.1 collective-permute-start.83
  1960.6 8.9 collective-permute-start.89
  2091.0 9.1 collective-permute-start.95
  (81 other events, 617.3 us)
where the time goes:
time: 2220 us; the launch traced here: 2210 us
  blocking collectives  1720 us (77%)
  starting transfers between devices  211 us (10%)
  waiting for transfers between devices  199 us (9%)
  other arithmetic  36.4 us (2%)
    psum x6, blocking collectives, precondition(): lax.psum(jnp.sum(weight * residual * result), ('gx', 'gy', 'gz'))  609 us
    psum x6, blocking collectives, precondition(): coarse_mid = lax.psum(restricted * own_row, ('gx', 'gy', 'gz'))  598 us
    psum x5, blocking collectives, body(): lax.psum(jnp.sum(weight * direction * image), ('gx', 'gy', 'gz'))  511 us
    ppermute x48, waiting for transfers between devices, extended(): lax.ppermute(head, axis, [((i + 1) % count, i) for i in range(ends)])  147 us
    ppermute x48, starting transfers between devices, extended(): lax.ppermute(tail, axis, [(i, (i + 1) % count) for i in range(ends)])  133 us
    ppermute x48, starting transfers between devices, extended(): lax.ppermute(head, axis, [((i + 1) % count, i) for i in range(ends)])  77.4 us
    ppermute x48, waiting for transfers between devices, extended(): lax.ppermute(tail, axis, [(i, (i + 1) % count) for i in range(ends)])  51.5 us
  transfers between devices with their start and end apart: 96, of which 59 were waited for; matrix products, arithmetic and copies ran while one was open for 0% of the time, Pallas kernels for 0%

commit v1 on v0

--- a/solution.py
+++ b/solution.py
@@ -169,7 +169,7 @@
     def precondition(residual):
         jacobi = residual / diagonal
         restricted = jnp.sum(weight * residual)
-        coarse_mid = lax.psum(restricted * own_row, ("gx", "gy", "gz"))
+        coarse_mid = lax.psum(lax.psum(restricted * own_row, ("gy", "gz")), "gx")
         coarse_value = jnp.dot(own_row, coarse_mid, precision=HIGHEST)
         result = jacobi + assemble((weight * coarse_value)[None])[0]
         return (result, lax.psum(jnp.sum(weight * residual * result), ("gx", "gy", "gz")))

time: 2220 us -> 2500 us (1.13)
  blocking collectives: 1720 us -> 2010 us
    psum x6 -> x12, blocking collectives: 598 us -> 918 us  [precondition(): coarse_mid = lax.psum(lax.psum(restricted * own_row, ('gy', 'gz')), 'gx')]
where the time goes in v1:
time: 2500 us; the launch traced here: 2480 us
  blocking collectives  2010 us (80%)
  starting transfers between devices  200 us (8%)
  waiting for transfers between devices  195 us (8%)
  other arithmetic  36.4 us (1%)
    psum x12, blocking collectives, precondition(): coarse_mid = lax.psum(lax.psum(restricted * own_row, ('gy', 'gz')), 'gx')  918 us
    psum x6, blocking collectives, precondition(): lax.psum(jnp.sum(weight * residual * result), ('gx', 'gy', 'gz'))  593 us
    psum x5, blocking collectives, body(): lax.psum(jnp.sum(weight * direction * image), ('gx', 'gy', 'gz'))  499 us
    ppermute x48, waiting for transfers between devices, extended(): lax.ppermute(head, axis, [((i + 1) % count, i) for i in range(ends)])  143 us
    ppermute x48, starting transfers between devices, extended(): lax.ppermute(tail, axis, [(i, (i + 1) % count) for i in range(ends)])  120 us
    ppermute x48, starting transfers between devices, extended(): lax.ppermute(head, axis, [((i + 1) % count, i) for i in range(ends)])  80.2 us
    ppermute x48, waiting for transfers between devices, extended(): lax.ppermute(tail, axis, [(i, (i + 1) % count) for i in range(ends)])  51.8 us
  transfers between devices with their start and end apart: 96, of which 59 were waited for; matrix products, arithmetic and copies ran while one was open for 0% of the time, Pallas kernels for 0%

profile of v1, /device:TPU:1, one launch (start us, length us, event | category | flops | bytes accessed | tf_op | source)
XLA Modules:
  0.0 2483.8 jit_solution(1696016323225068927)
XLA Ops:
  10.8 5.5 collective-permute-start.1
  103.5 112.0 %psum.168 = f32[512]{0:T(512)S(1)} all-reduce(f32[512]{0:T(512)S(1)} %broadcast_multiply_fusion.13), channel_id=1, replica_groups=mesh['gx'=8,'gy'=4,'gz'=16] {'gy','gz'}, use_global_device_ids=true, to_apply=%region_1.2 | all-reduce | flops 512 | bytes 4096 | tf_op jit(solution)/shard_map/psum | solution.py:172
  215.5 40.3 %psum.169 = f32[512]{0:T(512)S(1)} all-reduce(f32[512]{0:T(512)S(1)} %psum.168), channel_id=1, replica_groups=mesh['gx'=8,'gy'=4,'gz'=16] {'gx'}, use_global_device_ids=true, to_apply=%region_2.3 | all-reduce | flops 512 | bytes 4096 | tf_op jit(solution)/shard_map/psum | solution.py:172
  324.4 99.5 %all-reduce = (f32[]{:T(128)}, f32[]{:T(128)}) all-reduce(f32[]{:T(128)} %get-tuple-element.9, f32[]{:T(128)} %get-tuple-element.8), channel_id=1, replica_groups=mesh['gx'=8,'gy'=4,'gz'=16] {'gx','gy','gz'}, use_global_device_ids=true, to_apply=%region_4.5 | all-reduce | flops 2 | bytes 16 | tf_op jit(solution)/shard_map/psum | solution.py:175
  426.6 112.2 %psum.172 = f32[512]{0:T(512)S(1)} all-reduce(f32[512]{0:T(512)S(1)} %broadcast_multiply_fusion.12), channel_id=1, replica_groups=mesh['gx'=8,'gy'=4,'gz'=16] {'gy','gz'}, use_global_device_ids=true, to_apply=%region_8.9 | all-reduce | flops 512 | bytes 4096 | tf_op jit(solution)/shard_map/psum | solution.py:172
  538.7 40.3 %psum.173 = f32[512]{0:T(512)S(1)} all-reduce(f32[512]{0:T(512)S(1)} %psum.172), channel_id=1, replica_groups=mesh['gx'=8,'gy'=4,'gz'=16] {'gx'}, use_global_device_ids=true, to_apply=%region_9.10 | all-reduce | flops 512 | bytes 4096 | tf_op jit(solution)/shard_map/psum | solution.py:172
  605.1 98.6 %psum.174 = f32[]{:T(128)} all-reduce(f32[]{:T(128)} %get-tuple-element.36), channel_id=1, replica_groups=mesh['gx'=8,'gy'=4,'gz'=16] {'gx','gy','gz'}, use_global_device_ids=true, to_apply=%region_11.12 | all-reduce | flops 1 | bytes 8 | tf_op jit(solution)/shard_map/psum | solution.py:175
  734.8 99.7 %psum.175 = f32[]{:T(128)} all-reduce(f32[]{:T(128)} %get-tuple-element.34), channel_id=1, replica_groups=mesh['gx'=8,'gy'=4,'gz'=16] {'gx','gy','gz'}, use_global_device_ids=true, to_apply=%region_13.14 | all-reduce | flops 1 | bytes 8 | tf_op jit(solution)/shard_map/psum | solution.py:190
  837.2 113.0 %psum.176 = f32[512]{0:T(512)S(1)} all-reduce(f32[512]{0:T(512)S(1)} %broadcast_multiply_fusion.11), channel_id=1, replica_groups=mesh['gx'=8,'gy'=4,'gz'=16] {'gy','gz'}, use_global_device_ids=true, to_apply=%region_15.16 | all-reduce | flops 512 | bytes 4096 | tf_op jit(solution)/shard_map/psum | solution.py:172
  950.2 40.3 %psum.177 = f32[512]{0:T(512)S(1)} all-reduce(f32[512]{0:T(512)S(1)} %psum.176), channel_id=1, replica_groups=mesh['gx'=8,'gy'=4,'gz'=16] {'gx'}, use_global_device_ids=true, to_apply=%region_16.17 | all-reduce | flops 512 | bytes 4096 | tf_op jit(solution)/shard_map/psum | solution.py:172
  1016.4 98.9 %psum.178 = f32[]{:T(128)} all-reduce(f32[]{:T(128)} %get-tuple-element.30), channel_id=1, replica_groups=mesh['gx'=8,'gy'=4,'gz'=16] {'gx','gy','gz'}, use_global_device_ids=true, to_apply=%region_18.19 | all-reduce | flops 1 | bytes 8 | tf_op jit(solution)/shard_map/psum | solution.py:175
  1146.4 99.7 %psum.179 = f32[]{:T(128)} all-reduce(f32[]{:T(128)} %get-tuple-element.28), channel_id=1, replica_groups=mesh['gx'=8,'gy'=4,'gz'=16] {'gx','gy','gz'}, use_global_device_ids=true, to_apply=%region_20.21 | all-reduce | flops 1 | bytes 8 | tf_op jit(solution)/shard_map/psum | solution.py:190
  1248.8 113.0 %psum.180 = f32[512]{0:T(512)S(1)} all-reduce(f32[512]{0:T(512)S(1)} %broadcast_multiply_fusion.10), channel_id=1, replica_groups=mesh['gx'=8,'gy'=4,'gz'=16] {'gy','gz'}, use_global_device_ids=true, to_apply=%region_22.23 | all-reduce | flops 512 | bytes 4096 | tf_op jit(solution)/shard_map/psum | solution.py:172
  1361.8 40.3 %psum.181 = f32[512]{0:T(512)S(1)} all-reduce(f32[512]{0:T(512)S(1)} %psum.180), channel_id=1, replica_groups=mesh['gx'=8,'gy'=4,'gz'=16] {'gx'}, use_global_device_ids=true, to_apply=%region_23.24 | all-reduce | flops 512 | bytes 4096 | tf_op jit(solution)/shard_map/psum | solution.py:172
  1428.1 98.7 %psum.182 = f32[]{:T(128)} all-reduce(f32[]{:T(128)} %get-tuple-element.24), channel_id=1, replica_groups=mesh['gx'=8,'gy'=4,'gz'=16] {'gx','gy','gz'}, use_global_device_ids=true, to_apply=%region_25.26 | all-reduce | flops 1 | bytes 8 | tf_op jit(solution)/shard_map/psum | solution.py:175
  1557.9 99.7 %psum.183 = f32[]{:T(128)} all-reduce(f32[]{:T(128)} %get-tuple-element.22), channel_id=1, replica_groups=mesh['gx'=8,'gy'=4,'gz'=16] {'gx','gy','gz'}, use_global_device_ids=true, to_apply=%region_27.28 | all-reduce | flops 1 | bytes 8 | tf_op jit(solution)/shard_map/psum | solution.py:190
  1660.3 113.0 %psum.184 = f32[512]{0:T(512)S(1)} all-reduce(f32[512]{0:T(512)S(1)} %broadcast_multiply_fusion.9), channel_id=1, replica_groups=mesh['gx'=8,'gy'=4,'gz'=16] {'gy','gz'}, use_global_device_ids=true, to_apply=%region_29.30 | all-reduce | flops 512 | bytes 4096 | tf_op jit(solution)/shard_map/psum | solution.py:172
  1773.3 40.3 %psum.185 = f32[512]{0:T(512)S(1)} all-reduce(f32[512]{0:T(512)S(1)} %psum.184), channel_id=1, replica_groups=mesh['gx'=8,'gy'=4,'gz'=16] {'gx'}, use_global_device_ids=true, to_apply=%region_30.31 | all-reduce | flops 512 | bytes 4096 | tf_op jit(solution)/shard_map/psum | solution.py:172
  1839.5 98.9 %psum.186 = f32[]{:T(128)} all-reduce(f32[]{:T(128)} %get-tuple-element.18), channel_id=1, replica_groups=mesh['gx'=8,'gy'=4,'gz'=16] {'gx','gy','gz'}, use_global_device_ids=true, to_apply=%region_32.33 | all-reduce | flops 1 | bytes 8 | tf_op jit(solution)/shard_map/psum | solution.py:175
  1969.6 99.7 %psum.187 = f32[]{:T(128)} all-reduce(f32[]{:T(128)} %get-tuple-element.16), channel_id=1, replica_groups=mesh['gx'=8,'gy'=4,'gz'=16] {'gx','gy','gz'}, use_global_device_ids=true, to_apply=%region_34.35 | all-reduce | flops 1 | bytes 8 | tf_op jit(solution)/shard_map/psum | solution.py:190
  2072.0 113.0 %psum.188 = f32[512]{0:T(512)S(1)} all-reduce(f32[512]{0:T(512)S(1)} %broadcast_multiply_fusion.8), channel_id=1, replica_groups=mesh['gx'=8,'gy'=4,'gz'=16] {'gy','gz'}, use_global_device_ids=true, to_apply=%region_36.37 | all-reduce | flops 512 | bytes 4096 | tf_op jit(solution)/shard_map/psum | solution.py:172
  2185.0 40.3 %psum.189 = f32[512]{0:T(512)S(1)} all-reduce(f32[512]{0:T(512)S(1)} %psum.188), channel_id=1, replica_groups=mesh['gx'=8,'gy'=4,'gz'=16] {'gx'}, use_global_device_ids=true, to_apply=%region_37.38 | all-reduce | flops 512 | bytes 4096 | tf_op jit(solution)/shard_map/psum | solution.py:172
  2251.2 98.7 %psum.190 = f32[]{:T(128)} all-reduce(f32[]{:T(128)} %get-tuple-element.12), channel_id=1, replica_groups=mesh['gx'=8,'gy'=4,'gz'=16] {'gx','gy','gz'}, use_global_device_ids=true, to_apply=%region_39.40 | all-reduce | flops 1 | bytes 8 | tf_op jit(solution)/shard_map/psum | solution.py:175
  2381.8 99.7 %psum.191 = f32[]{:T(128)} all-reduce(f32[]{:T(128)} %fusion.92), channel_id=1, replica_groups=mesh['gx'=8,'gy'=4,'gz'=16] {'gx','gy','gz'}, use_global_device_ids=true, to_apply=%region_41.42 | all-reduce | flops 1 | bytes 8 | tf_op jit(solution)/shard_map/psum | solution.py:190
  (443 shorter events, 450.5 us)
Async XLA Ops:
  6.2 10.1 collective-permute-start
  58.3 10.6 collective-permute-start.11
  87.6 10.1 collective-permute-start.16
  92.5 9.1 collective-permute-start.17
  257.2 10.3 collective-permute-start.24
  275.7 9.0 collective-permute-start.28
  277.4 9.2 collective-permute-start.29
  278.9 9.0 collective-permute-start.22
  282.9 8.9 collective-permute-start.23
  314.0 9.1 collective-permute-start.35
  594.8 8.9 collective-permute-start.41
  720.7 8.9 collective-permute-start.46
  724.4 9.1 collective-permute-start.47
  1006.0 9.1 collective-permute-start.53
  1132.3 8.9 collective-permute-start.58
  1136.0 9.1 collective-permute-start.59
  1417.6 9.1 collective-permute-start.65
  1543.8 8.9 collective-permute-start.70
  1547.5 9.1 collective-permute-start.71
  1829.1 9.1 collective-permute-start.77
  1955.5 8.9 collective-permute-start.82
  1959.2 9.1 collective-permute-start.83
  2240.7 9.1 collective-permute-start.89
  2370.6 9.1 collective-permute-start.95
  (81 other events, 700.7 us)
